TPU v7x, 512 devices: a whole 4x8x8 slice. The times are simulated.
512 devices in a mesh: layer: 8 (over z), row: 64 (over y, x, core).
Axes of the slice: x: 4, y: 8, z: 8, core: 2. Of those that a mesh axis runs over, the one named last changes fastest.
Arguments:
- left_factors: bfloat16 [8, 65536, 128], P('layer', 'row'), may hold values from -0.1875 to 0.1875
- right_factors: bfloat16 [8, 65536, 128], P('layer', 'row'), may hold values from -0.1875 to 0.1875
- sketch: bfloat16 [65536, 128], P('row'), may hold values from -0.1875 to 0.1875
- row_basis: bfloat16 [65536, 128], P('row'), may hold values from -0.4375 to 0.4375
- inverse_diag: bfloat16 [65536, 1024], P('row'), may hold values from -0.0625 to 1.44125, as said below
- right_side: bfloat16 [65536, 4096], P('row', 'layer'), may hold values from -6 to 6
- incoming: float32 [128, 4096], P(None, 'layer'), may hold values from -6 to 6
Outputs:
- solution: bfloat16 [65536, 4096], P('row', 'layer')
Inputs may be any that keep to these rules, and one draw needn't show every extreme that they name: `inverse_diag`: each block of 1024 rows is the inverse of that row group's diagonal tile.
All inputs are finite; a program needn't handle non-finite values.
Results may differ from a plain program's by a relative error of at most 0.0095.
Values may be sent and summed in bfloat16 or wider, within the bound.
A program may use at most 128 MiB of HBM per device.

v0:
```python
import jax
import jax.numpy as jnp
from jax import lax
from jax.sharding import PartitionSpec as P


def shifted(value, axis, steps):
    count = lax.axis_size(axis)
    leading, last = (max(0, -steps), min(count, count - steps))
    return lax.ppermute(value, axis, [(source, source + steps) for source in range(leading, last)])


def entering(value, axis, combine, identity):
    count, here = (lax.axis_size(axis), lax.axis_index(axis))
    everything = jax.tree.map(lambda part: lax.all_gather(part, axis), value)
    start = jax.tree.map(
        lambda part, zero: jnp.broadcast_to(jnp.asarray(zero, part.dtype), part.shape),
        value,
        identity,
    )

    def lap(k, before):
        reached = k < here
        new = combine(before, jax.tree.map(lambda part: part[k], everything))
        return jax.tree.map(lambda a, b: jnp.where(reached, a, b), new, before)

    return lax.fori_loop(0, count, lap, start)


def project(basis, vectors):
    return lax.dot_general(
        basis, vectors, (((0,), (0,)), ((), ())), preferred_element_type=jnp.float32
    )


def body(left_factors, right_factors, sketch, row_basis, inverse_diag, right_side, incoming):
    full = lax.Precision.HIGHEST
    rank = sketch.shape[1]
    width = right_side.shape[1]
    core = project(right_factors[0], sketch).astype(jnp.bfloat16)
    partial_range = -jnp.dot(left_factors[0], core, preferred_element_type=jnp.float32)
    tile_range = lax.psum(partial_range, "layer").astype(jnp.bfloat16)
    applied = jnp.dot(inverse_diag, right_side, preferred_element_type=jnp.float32).astype(
        jnp.bfloat16
    )
    gain = jnp.dot(inverse_diag, tile_range, preferred_element_type=jnp.float32).astype(
        jnp.bfloat16
    )

    def combine(earlier, later):
        return (
            jnp.dot(later[0], earlier[0], precision=full),
            jnp.dot(later[0], earlier[1], precision=full) + later[1],
        )

    identity = (jnp.eye(rank, dtype=jnp.float32), jnp.zeros((rank, width), jnp.float32))
    joined = jnp.concatenate([applied, gain], axis=1)
    carried = shifted(joined, "row", 1)
    step_map = -project(row_basis, carried[:, width:])
    step_shift = project(row_basis, carried[:, :width])
    first_group = lax.axis_index("row") == 0
    step_shift = jnp.where(first_group, incoming, step_shift)
    prefix = entering((step_map, step_shift), "row", combine, identity)
    coupled = jnp.dot(step_map, prefix[1], precision=full) + step_shift
    result = applied.astype(jnp.float32) - jnp.dot(
        gain.astype(jnp.float32), coupled, precision=full
    )
    return result.astype(jnp.bfloat16)


def solution(mesh):
    return jax.shard_map(
        body,
        mesh=mesh,
        in_specs=(
            P("layer", "row", None),
            P("layer", "row", None),
            P("row", None),
            P("row", None),
            P("row", None),
            P("row", "layer"),
            P(None, "layer"),
        ),
        out_specs=P("row", "layer"),
        check_vma=False,
    )
```

profile of v0, /device:TPU:1, one launch (start us, length us, event | category | flops | bytes accessed | tf_op | source)
XLA Modules:
  0.0 390.4 jit_solution(16829505180996091301)
XLA Ops:
  6.5 1.8 fusion.8
  8.3 36.2 %all-reduce.1 = bf16[1024,128]{0,1:T(8,128)(2,1)S(1)} all-reduce(f32[1024,128]{0,1:T(8,128)S(1)} %fusion.8), channel_id=1, replica_groups=mesh['layer'=8,'row'=64] {'layer'}, use_global_device_ids=true, to_apply=%region_0.0 | all-reduce | flops 131072 | bytes 786432 | tf_op jit(solution)/shard_map/psum | solution.py:42
  47.2 10.9 %collective-permute-start = (bf16[1024,640]{0,1:T(8,128)(2,1)S(1)}, bf16[1024,640]{0,1:T(8,128)(2,1)S(1)}, u32[]{:S(2)}, u32[]{:S(2)}) collective-permute-start(bf16[1024,640]{0,1:T(8,128)(2,1)S(1)} %pad_maximum_fusion), channel_id=1, source_target_pairs={{0,1},{1,2},{2,3},{3,4},{4,5},{5,6},{6,7},{7,8},{8,9},{9,10},{10,1... | collective-permute-start | bytes 3932168 | tf_op jit(solution)/shard_map/ppermute | solution.py:10
  58.1 14.5 %collective-permute-done = bf16[1024,640]{0,1:T(8,128)(2,1)S(1)} collective-permute-done((bf16[1024,640]{0,1:T(8,128)(2,1)S(1)}, bf16[1024,640]{0,1:T(8,128)(2,1)S(1)}, u32[]{:S(2)}, u32[]{:S(2)}) %collective-permute-start) | collective-permute-done | bytes 1310752 | tf_op jit(solution)/shard_map/ppermute | solution.py:10
  74.7 2.4 fusion.9
  77.1 77.1 %all-gather.5.cloned.1.call-done = f32[8192,128]{0,1:T(8,128)} async-done(((f32[128,128]{0,1:T(8,128)}), f32[8192,128]{0,1:T(8,128)}) %all-gather.5.cloned.1.call-update) | async-done | bytes 4194320 | tf_op jit(solution)/shard_map/all_gather | solution.py:15
  154.2 5.6 %copy.14 = f32[8192,128]{1,0:T(8,128)} copy(f32[8192,128]{0,1:T(8,128)} %all-gather.5.cloned.1.call-done) | data formatting | bytes 8388608
  159.9 108.3 %all-gather.7.cloned.1.call-done = f32[8192,512]{0,1:T(8,128)} async-done(((f32[128,512]{0,1:T(8,128)}), f32[8192,512]{0,1:T(8,128)}) %all-gather.7.cloned.1.call-update) | async-done | bytes 16777232 | tf_op jit(solution)/shard_map/all_gather | solution.py:15
  268.2 17.4 %copy.15 = f32[8192,512]{1,0:T(8,128)} copy(f32[8192,512]{0,1:T(8,128)} %all-gather.7.cloned.1.call-done) | data formatting | bytes 33554432
  285.6 91.2 %while.14 = (s32[]{:T(128)}, f32[128,512]{1,0:T(8,128)S(1)}, s32[]{:T(128)}, f32[64,128,128]{2,1,0:T(8,128)}, f32[64,128,512]{2,1,0:T(8,128)}, /*index=5*/s32[]{:T(128)}, s32[]{:T(128)}) while((s32[]{:T(128)}, f32[128,512]{1,0:T(8,128)S(1)}, s32[]{:T(128)}, f32[64,128,128]{2,1,0:T(8,128)}, f32[64,128,512]{2,1,0:T(8,128)}, ...), condition=%wide.region_2.3_spmd.clone, body=%wide.region_1.2_spmd.clone.sunk | while | flops 100925440 | bytes 1641055 | solution.py:27
  288.5 1.4 fusion.32
  289.9 1.4 fusion.32
  291.3 1.4 fusion.32
  294.2 1.4 fusion.32
  297.0 1.4 fusion.32
  302.7 1.4 fusion.32
  304.1 1.4 fusion.32
  305.6 1.4 fusion.32
  311.3 1.4 fusion.32
  317.0 1.4 fusion.32
  319.8 1.4 fusion.32
  325.5 1.4 fusion.32
  334.1 1.4 fusion.32
  336.9 1.4 fusion.32
  348.3 1.4 fusion.32
  351.2 1.4 fusion.32
  362.6 1.4 fusion.32
  365.4 1.4 fusion.32
  375.4 1.4 fusion.32
  376.8 1.5 convolution_add_fusion.1
  378.3 2.9 subtract_convert_fusion
  381.3 2.3 copy.12
  (133 shorter events, 67.5 us)
Async XLA Ops:
  6.5 38.0 %copy-start = (bf16[1024,1024]{1,0:T(8,128)(2,1)S(1)}, bf16[1024,1024]{1,0:T(8,128)(2,1)}, u32[]{:S(2)}) copy-start(bf16[1024,1024]{1,0:T(8,128)(2,1)} %param.13) | copy-start | bytes 6291460
  6.5 147.7 %all-gather.5.cloned.1.call-start = ((), (), s32[]{:S(2)}) async-start(), calls=%async_computation | async-start | bytes 4259840 | tf_op jit(solution)/shard_map/all_gather | solution.py:15
  44.5 1.2 copy-start.6
  45.8 1.3 copy-start.1
  47.1 25.6 %copy-start.4 = (bf16[1024,128]{1,0:T(8,128)(2,1)S(1)}, bf16[1024,128]{1,0:T(8,128)(2,1)}, u32[]{:S(2)}) copy-start(bf16[1024,128]{1,0:T(8,128)(2,1)} %param.12) | copy-start | bytes 786436
  47.1 26.8 %copy-start.3 = (f32[128,512]{1,0:T(8,128)S(1)}, f32[128,512]{1,0:T(8,128)}, u32[]{:S(2)}) copy-start(f32[128,512]{1,0:T(8,128)} %param.15) | copy-start | bytes 786436
  47.2 25.4 %collective-permute-start = (bf16[1024,640]{0,1:T(8,128)(2,1)S(1)}, bf16[1024,640]{0,1:T(8,128)(2,1)S(1)}, u32[]{:S(2)}, u32[]{:S(2)}) collective-permute-start(bf16[1024,640]{0,1:T(8,128)(2,1)S(1)} %pad_maximum_fusion), channel_id=1, source_target_pairs={{0,1},{1,2},{2,3},{3,4},{4,5},{5,6},{6,7},{7,8},{8,9},{9,10},{10,1... | collective-permute-start | bytes 3932168 | tf_op jit(solution)/shard_map/ppermute | solution.py:10
  72.7 1.1 copy-start.5
  73.8 194.4 %all-gather.7.cloned.1.call-start = ((), (), s32[]{:S(2)}) async-start(), calls=%async_computation.1 | async-start | bytes 17039360 | tf_op jit(solution)/shard_map/all_gather | solution.py:15
  285.6 91.2 %copy-start.2 = (f32[128,128]{1,0:T(8,128)S(1)}, f32[128,128]{1,0:T(8,128)}, u32[]{:S(2)}) copy-start(f32[128,128]{1,0:T(8,128)} %convolution_negate_fusion.1) | copy-start | bytes 196612
Sparse Core Ops, SparseCore 0:
  73.9 80.2 all-gather.4
  157.5 110.6 all-gather.6
where the time goes:
time: 392 us; the launch traced here: 390 us
  waiting for transfers between devices  200 us (51%)
  matrix products  99.5 us (25%)
  blocking collectives  36.2 us (9%)
  local copies, waits for them, and re-layouts  27.8 us (7%)
  between operations  13.5 us (3%)
  starting transfers between devices  10.9 us (3%)
    all_gather x2, waiting for transfers between devices, entering(): everything = jax.tree.map(lambda part: lax.all_gather(part, axis), value)  185 us
    dot_general x64, matrix products, combine(): jnp.dot(later[0], earlier[1], precision=full) + later[1]  87.6 us
    psum x1, blocking collectives, body(): tile_range = lax.psum(partial_range, 'layer').astype(jnp.bfloat16)  36.2 us
    unnamed x17, local copies, waits for them, and re-layouts  24.3 us
    ppermute x1, waiting for transfers between devices, shifted(): lax.ppermute(value, axis, [(source, source + steps) for source in range(l...  14.5 us
    ppermute x1, starting transfers between devices, shifted(): lax.ppermute(value, axis, [(source, source + steps) for source in range(l...  10.9 us
  transfers between devices with their start and end apart: 3, of which 3 were waited for; matrix products, arithmetic and copies ran while one was open for 2% of the time, Pallas kernels for 0%

commit v1 on v0

--- a/solution.py
+++ b/solution.py
@@ -39,7 +39,7 @@
     width = right_side.shape[1]
     core = project(right_factors[0], sketch).astype(jnp.bfloat16)
     partial_range = -jnp.dot(left_factors[0], core, preferred_element_type=jnp.float32)
-    tile_range = lax.psum(partial_range, "layer").astype(jnp.bfloat16)
+    tile_range = jnp.sum(lax.all_gather(partial_range, "layer"), axis=0).astype(jnp.bfloat16)
     applied = jnp.dot(inverse_diag, right_side, preferred_element_type=jnp.float32).astype(
         jnp.bfloat16
     )

time: 392 us -> 420 us (1.071)
  waiting for transfers between devices: 200 us -> 262 us
  blocking collectives: 36.2 us -> 0 us
  starting transfers between devices: 10.9 us -> 3.91 us
  local copies, waits for them, and re-layouts: 27.8 us -> 33.6 us
    all_gather x0 -> x1, waiting for transfers between devices: none -> 61.2 us  [body(): lax.all_gather(partial_range, 'layer')]
    psum x1 -> x0, blocking collectives: 36.2 us -> none  [body(): tile_range = lax.psum(partial_range, 'layer').astype(jnp.bfloat16)]
    ppermute x1, starting transfers between devices: 10.9 us -> 3.83 us  [shifted(): lax.ppermute(value, axis, [(source, source + steps) for source in range(l...]
    unnamed x17 -> x16, local copies, waits for them, and re-layouts: 24.3 us -> 30.1 us
  transfers between devices with their start and end apart: 3 -> 4, of which waited for: 3 -> 4; matrix products, arithmetic and copies ran while one was open for 2% -> 3% of each run, Pallas kernels for 0% -> 0%
where the time goes in v1:
time: 420 us; the launch traced here: 418 us
  waiting for transfers between devices  262 us (62%)
  matrix products  101 us (24%)
  local copies, waits for them, and re-layouts  33.6 us (8%)
  between operations  13.2 us (3%)
    all_gather x2, waiting for transfers between devices, entering(): everything = jax.tree.map(lambda part: lax.all_gather(part, axis), value)  186 us
    dot_general x64, matrix products, combine(): jnp.dot(later[0], earlier[1], precision=full) + later[1]  87.6 us
    all_gather x1, waiting for transfers between devices, body(): lax.all_gather(partial_range, 'layer')  61.2 us
    unnamed x16, local copies, waits for them, and re-layouts  30.1 us
    ppermute x1, waiting for transfers between devices, shifted(): lax.ppermute(value, axis, [(source, source + steps) for source in range(l...  14.5 us
  transfers between devices with their start and end apart: 4, of which 4 were waited for; matrix products, arithmetic and copies ran while one was open for 3% of the time, Pallas kernels for 0%

profile of v1, /device:TPU:1, one launch (start us, length us, event | category | flops | bytes accessed | tf_op | source)
XLA Modules:
  0.0 417.9 jit_solution(14221680552633576290)
XLA Ops:
  6.5 2.6 fusion.8
  9.2 2.5 convolution_convert_fusion
  11.7 61.2 %all-gather.7.cloned.1.call-done = f32[8192,128]{0,1:T(8,128)} async-done(((f32[1024,128]{0,1:T(8,128)}), f32[8192,128]{0,1:T(8,128)}) %all-gather.7.cloned.1.call-update) | async-done | bytes 4194320 | tf_op jit(solution)/shard_map/all_gather | solution.py:42
  73.0 5.4 %copy.21 = f32[16,8,8,1024]{3,2,1,0:T(8,128)S(1)} copy(f32[16,8,8,1024]{3,1,2,0:T(8,128)} %bitcast.44) | data formatting | bytes 8388608
  81.1 3.8 collective-permute-start
  84.9 14.5 %collective-permute-done = bf16[1024,640]{0,1:T(8,128)(2,1)S(1)} collective-permute-done((bf16[1024,640]{0,1:T(8,128)(2,1)S(1)}, bf16[1024,640]{0,1:T(8,128)(2,1)S(1)}, u32[]{:S(2)}, u32[]{:S(2)}) %collective-permute-start) | collective-permute-done | bytes 1310752 | tf_op jit(solution)/shard_map/ppermute | solution.py:10
  101.5 2.4 fusion.9
  103.9 78.2 %all-gather.9.cloned.1.call-done = f32[8192,128]{0,1:T(8,128)} async-done(((f32[128,128]{0,1:T(8,128)}), f32[8192,128]{0,1:T(8,128)}) %all-gather.9.cloned.1.call-update) | async-done | bytes 4194320 | tf_op jit(solution)/shard_map/all_gather | solution.py:15
  182.1 5.6 %copy.19 = f32[8192,128]{1,0:T(8,128)} copy(f32[8192,128]{0,1:T(8,128)} %all-gather.9.cloned.1.call-done) | data formatting | bytes 8388608
  187.7 108.3 %all-gather.11.cloned.1.call-done = f32[8192,512]{0,1:T(8,128)} async-done(((f32[128,512]{0,1:T(8,128)}), f32[8192,512]{0,1:T(8,128)}) %all-gather.11.cloned.1.call-update) | async-done | bytes 16777232 | tf_op jit(solution)/shard_map/all_gather | solution.py:15
  296.0 17.4 %copy.20 = f32[8192,512]{1,0:T(8,128)} copy(f32[8192,512]{0,1:T(8,128)} %all-gather.11.cloned.1.call-done) | data formatting | bytes 33554432
  313.5 91.2 %while.14 = (s32[]{:T(128)}, f32[128,512]{1,0:T(8,128)S(1)}, s32[]{:T(128)}, f32[64,128,128]{2,1,0:T(8,128)}, f32[64,128,512]{2,1,0:T(8,128)}, /*index=5*/s32[]{:T(128)}, s32[]{:T(128)}) while((s32[]{:T(128)}, f32[128,512]{1,0:T(8,128)S(1)}, s32[]{:T(128)}, f32[64,128,128]{2,1,0:T(8,128)}, f32[64,128,512]{2,1,0:T(8,128)}, ...), condition=%wide.region_2.3_spmd.clone, body=%wide.region_1.2_spmd.clone.sunk | while | flops 100925440 | bytes 1641055 | solution.py:27
  313.5 1.4 fusion.32
  316.3 1.4 fusion.32
  322.0 1.4 fusion.32
  323.4 1.4 fusion.32
  324.9 1.4 fusion.32
  327.7 1.4 fusion.32
  330.6 1.4 fusion.32
  336.3 1.4 fusion.32
  337.7 1.4 fusion.32
  339.1 1.4 fusion.32
  342.0 1.4 fusion.32
  344.8 1.4 fusion.32
  350.5 1.4 fusion.32
  353.4 1.4 fusion.32
  367.6 1.4 fusion.32
  381.9 1.4 fusion.32
  396.1 1.4 fusion.32
  404.6 1.5 convolution_add_fusion.1
  406.2 2.9 subtract_convert_fusion
  409.1 2.3 copy.17
  (135 shorter events, 70.3 us)
Async XLA Ops:
  6.5 2.6 copy-start
  6.5 66.4 %all-gather.7.cloned.1.call-start = ((), (), s32[]{:S(2)}) async-start(), calls=%async_computation | async-start | bytes 4718592 | tf_op jit(solution)/shard_map/all_gather | solution.py:42
  9.1 173.0 %all-gather.9.cloned.1.call-start = ((), (), s32[]{:S(2)}) async-start(), calls=%async_computation.1 | async-start | bytes 4259840 | tf_op jit(solution)/shard_map/all_gather | solution.py:15
  79.4 20.0 %copy-start.4 = (bf16[1024,128]{1,0:T(8,128)(2,1)S(1)}, bf16[1024,128]{1,0:T(8,128)(2,1)}, u32[]{:S(2)}) copy-start(bf16[1024,128]{1,0:T(8,128)(2,1)} %param.12) | copy-start | bytes 786436
  80.3 0.7 copy-start.1
  80.3 20.3 %copy-start.3 = (f32[128,512]{1,0:T(8,128)S(1)}, f32[128,512]{1,0:T(8,128)}, u32[]{:S(2)}) copy-start(f32[128,512]{1,0:T(8,128)} %param.15) | copy-start | bytes 786436
  81.1 18.4 %collective-permute-start = (bf16[1024,640]{0,1:T(8,128)(2,1)S(1)}, bf16[1024,640]{0,1:T(8,128)(2,1)S(1)}, u32[]{:S(2)}, u32[]{:S(2)}) collective-permute-start(bf16[1024,640]{0,1:T(8,128)(2,1)S(1)} %pad_maximum_fusion), channel_id=1, source_target_pairs={{0,1},{1,2},{2,3},{3,4},{4,5},{5,6},{6,7},{7,8},{8,9},{9,10},{10,1... | collective-permute-start | bytes 3932168 | tf_op jit(solution)/shard_map/ppermute | solution.py:10
  99.4 1.1 copy-start.5
  100.6 195.4 %all-gather.11.cloned.1.call-start = ((), (), s32[]{:S(2)}) async-start(), calls=%async_computation.2 | async-start | bytes 17039360 | tf_op jit(solution)/shard_map/all_gather | solution.py:15
  313.5 91.2 %copy-start.2 = (f32[128,128]{1,0:T(8,128)S(1)}, f32[128,128]{1,0:T(8,128)}, u32[]{:S(2)}) copy-start(f32[128,128]{1,0:T(8,128)} %convolution_negate_fusion.1) | copy-start | bytes 196612
Sparse Core Ops, SparseCore 0:
  9.4 63.4 all-gather.6
  100.7 81.3 all-gather.8
  185.3 110.6 all-gather.10
